TPU v7x, 32 devices: a whole 2x2x4 slice. The times are simulated.
32 devices in a mesh: dp: 2 (over x), fsdp: 16 (over z, y, core).
Axes of the slice: x: 2, y: 2, z: 4, core: 2. Of those that a mesh axis runs over, the one named last changes fastest.
Arguments:
- activations: bfloat16 [2, 32, 128, 768], P(None, ('dp', 'fsdp')), may hold values from -6 to 6
- pair_repr: bfloat16 [2, 32, 128, 128, 256], P(None, ('dp', 'fsdp')), may hold values from -6 to 6
- cotangent: bfloat16 [2, 32, 128, 768], P(None, ('dp', 'fsdp')), may hold values from -6 to 6
- buckets: int32 [2, 32], P(None, ('dp', 'fsdp')), may hold values from 32 to 128, as said below
- pad_mask: int32 [2, 32, 128], P(None, ('dp', 'fsdp')), may hold values 0 or 1
- cath_ids: int32 [2, 32], P(None, ('dp', 'fsdp')), may hold values from 0 to 1023
- time_bins: int32 [2, 32], P(None, ('dp', 'fsdp')), may hold values from 0 to 999
- cath_table: bfloat16 [1024, 768], P(None, 'fsdp'), may hold values from -4.1875 to 4.1875
- time_table: bfloat16 [1000, 768], P(None, 'fsdp'), may hold values from -4.1875 to 4.1875
- cond_attn: bfloat16 [768, 2304], P('fsdp'), may hold values from -0.21875 to 0.21875
- cond_ffn: bfloat16 [768, 2304], P('fsdp'), may hold values from -0.21875 to 0.21875
- norm_attn: bfloat16 [768], P('fsdp'), may hold values from 0.5 to 1.5
- norm_ffn: bfloat16 [768], P('fsdp'), may hold values from 0.5 to 1.5
- pair_gain: bfloat16 [256], P('fsdp'), may hold values from 0.5 to 1.5
- qkv_weight: bfloat16 [768, 2304], P('fsdp'), may hold values from -0.21875 to 0.21875
- out_weight: bfloat16 [768, 768], P('fsdp'), may hold values from -0.875 to 0.875
- pair_weight: bfloat16 [256, 12], P('fsdp'), may hold values from -0.375 to 0.375
- gateup_weight: bfloat16 [768, 6144], P('fsdp'), may hold values from -0.21875 to 0.21875
- down_weight: bfloat16 [3072, 768], P('fsdp'), may hold values from -0.109375 to 0.109375
Outputs:
- block_out: bfloat16 [2, 32, 128, 768], P(None, ('dp', 'fsdp'))
- grad_input: bfloat16 [2, 32, 128, 768], P(None, ('dp', 'fsdp'))
- grad_pair: bfloat16 [2, 32, 128, 128, 256], P(None, ('dp', 'fsdp'))
- grad_cath: float32 [1024, 768], P(None, 'fsdp')
- grad_time: float32 [1000, 768], P(None, 'fsdp')
- grad_cond_attn: float32 [768, 2304], P('fsdp')
- grad_cond_ffn: float32 [768, 2304], P('fsdp')
- grad_norm_attn: float32 [768], P('fsdp')
- grad_norm_ffn: float32 [768], P('fsdp')
- grad_pair_gain: float32 [256], P('fsdp')
- grad_qkv_weight: float32 [768, 2304], P('fsdp')
- grad_out_weight: float32 [768, 768], P('fsdp')
- grad_pair_weight: float32 [256, 12], P('fsdp')
- grad_gateup_weight: float32 [768, 6144], P('fsdp')
- grad_down_weight: float32 [3072, 768], P('fsdp')
Inputs may be any that keep to these rules, and one draw needn't show every extreme that they name: `buckets`: each bucket size is 128, 64 or 32.
All inputs are finite; a program needn't handle non-finite values. No bound on the sum of `pad_mask` on one device may be relied on, other than what follows from the above.
Results may differ from a plain program's by a relative error of at most 0.024.
Values may be sent and summed in bfloat16 or wider, within the bound.
No kernel may reach another device: no remote copies, remote signals or barrier semaphores. Data moves between devices by JAX's collectives and lax.ppermute only.
A program may use at most 256 MiB of HBM per device.

v0:
```python
import math

import jax
import jax.numpy as jnp
from jax import lax
from jax.sharding import PartitionSpec as P


def normed_parts(values):
    center = values - jnp.mean(values, axis=-1, keepdims=True)
    inverse = lax.rsqrt(jnp.mean(center * center, axis=-1, keepdims=True) + 1e-05)
    return (center * inverse, inverse)


def normed_back(grad_hat, normed, inverse):
    return inverse * (
        grad_hat
        - jnp.mean(grad_hat, axis=-1, keepdims=True)
        - normed * jnp.mean(grad_hat * normed, axis=-1, keepdims=True)
    )


def silu_slope(values):
    sigma = jax.nn.sigmoid(values)
    return sigma * (1.0 + values * (1.0 - sigma))


def contract(former, latter, former_dim, latter_dim):
    return lax.dot_general(
        former,
        latter,
        (((former_dim,), (latter_dim,)), ((), ())),
        preferred_element_type=jnp.float32,
    )


def layer_forward(weights, chain_act, chain_pair, live_keys, cath_id, time_bin):
    (
        cath_table,
        time_table,
        cond_attn,
        cond_ffn,
        norm_attn,
        norm_ffn,
        pair_gain,
        qkv_weight,
        out_weight,
        pair_weight,
        gateup_weight,
        down_weight,
    ) = weights
    model_width = chain_act.shape[-1]
    length = chain_act.shape[0]
    head_count = pair_weight.shape[1]
    head_size = model_width // head_count
    hidden_width = down_weight.shape[0]
    score_scale = 1.0 / math.sqrt(head_size)
    cath_hot = (lax.broadcasted_iota(jnp.int32, (1, cath_table.shape[0]), 1) == cath_id).astype(
        jnp.bfloat16
    )
    time_hot = (lax.broadcasted_iota(jnp.int32, (1, time_table.shape[0]), 1) == time_bin).astype(
        jnp.bfloat16
    )
    cond_raw = jnp.dot(cath_hot, cath_table, preferred_element_type=jnp.float32) + jnp.dot(
        time_hot, time_table, preferred_element_type=jnp.float32
    )
    cond_act = jax.nn.silu(cond_raw).astype(jnp.bfloat16)
    mod_attn = jnp.dot(cond_act, cond_attn, preferred_element_type=jnp.float32)
    mod_ffn = jnp.dot(cond_act, cond_ffn, preferred_element_type=jnp.float32)
    row_live = live_keys.astype(jnp.float32)[:, None]
    attn_hat, attn_inv = normed_parts(chain_act)
    normed_attn = (
        attn_hat * norm_attn * (1.0 + mod_attn[:, model_width : 2 * model_width])
        + mod_attn[:, :model_width]
    ).astype(jnp.bfloat16)
    projected = jnp.dot(normed_attn, qkv_weight, preferred_element_type=jnp.float32).astype(
        jnp.bfloat16
    )
    query_heads = projected[:, :model_width].reshape(length, head_count, head_size)
    key_heads = projected[:, model_width : 2 * model_width].reshape(length, head_count, head_size)
    value_heads = projected[:, 2 * model_width :].reshape(length, head_count, head_size)
    pair_hat, pair_inv = normed_parts(chain_pair.astype(jnp.float32))
    pair_in = (pair_hat * pair_gain).astype(jnp.bfloat16)
    pair_bias = jnp.einsum("ijc,ch->hij", pair_in, pair_weight, preferred_element_type=jnp.float32)
    scores = (
        jnp.einsum("ihd,jhd->hij", query_heads, key_heads, preferred_element_type=jnp.float32)
        * score_scale
        + pair_bias
    )
    scores = jnp.where(live_keys[None, None, :], scores, -1000000000.0)
    attn_probs = jax.nn.softmax(scores, axis=-1)
    probs_low = attn_probs.astype(jnp.bfloat16)
    attn_mixed = (
        jnp.einsum("hij,jhd->ihd", probs_low, value_heads, preferred_element_type=jnp.float32)
        .reshape(length, model_width)
        .astype(jnp.bfloat16)
    )
    branch_attn = jnp.dot(attn_mixed, out_weight, preferred_element_type=jnp.float32)
    after_attn = chain_act + mod_attn[:, 2 * model_width :] * row_live * branch_attn
    ffn_hat, ffn_inv = normed_parts(after_attn)
    normed_ffn = (
        ffn_hat * norm_ffn * (1.0 + mod_ffn[:, model_width : 2 * model_width])
        + mod_ffn[:, :model_width]
    ).astype(jnp.bfloat16)
    gate_up = jnp.dot(normed_ffn, gateup_weight, preferred_element_type=jnp.float32).astype(
        jnp.bfloat16
    )
    gate_part = gate_up[:, :hidden_width].astype(jnp.float32)
    up_part = gate_up[:, hidden_width:].astype(jnp.float32)
    hidden = (jax.nn.silu(gate_part) * up_part).astype(jnp.bfloat16)
    branch_ffn = jnp.dot(hidden, down_weight, preferred_element_type=jnp.float32)
    output = after_attn + mod_ffn[:, 2 * model_width :] * row_live * branch_ffn
    saved = (
        cath_hot,
        time_hot,
        cond_raw,
        cond_act,
        mod_attn,
        mod_ffn,
        row_live,
        attn_hat,
        attn_inv,
        normed_attn,
        query_heads,
        key_heads,
        value_heads,
        pair_hat,
        pair_inv,
        pair_in,
        attn_probs,
        probs_low,
        attn_mixed,
        branch_attn,
        ffn_hat,
        ffn_inv,
        normed_ffn,
        gate_part,
        up_part,
        hidden,
        branch_ffn,
    )
    return (output, saved)


def layer_backward(weights, saved, grad_out):
    (
        cath_table,
        time_table,
        cond_attn,
        cond_ffn,
        norm_attn,
        norm_ffn,
        pair_gain,
        qkv_weight,
        out_weight,
        pair_weight,
        gateup_weight,
        down_weight,
    ) = weights
    (
        cath_hot,
        time_hot,
        cond_raw,
        cond_act,
        mod_attn,
        mod_ffn,
        row_live,
        attn_hat,
        attn_inv,
        normed_attn,
        query_heads,
        key_heads,
        value_heads,
        pair_hat,
        pair_inv,
        pair_in,
        attn_probs,
        probs_low,
        attn_mixed,
        branch_attn,
        ffn_hat,
        ffn_inv,
        normed_ffn,
        gate_part,
        up_part,
        hidden,
        branch_ffn,
    ) = saved
    model_width = grad_out.shape[-1]
    length = grad_out.shape[0]
    head_count = pair_weight.shape[1]
    head_size = model_width // head_count
    score_scale = 1.0 / math.sqrt(head_size)
    highest = lax.Precision.HIGHEST
    grad_branch_ffn = (mod_ffn[:, 2 * model_width :] * row_live * grad_out).astype(jnp.bfloat16)
    grad_gate_ffn = jnp.sum(row_live * branch_ffn * grad_out, axis=0, keepdims=True)
    grad_down = contract(hidden, grad_branch_ffn, 0, 0)
    grad_hidden = contract(grad_branch_ffn, down_weight, 1, 1)
    grad_gate_part = grad_hidden * up_part * silu_slope(gate_part)
    grad_up_part = grad_hidden * jax.nn.silu(gate_part)
    grad_gate_up = jnp.concatenate([grad_gate_part, grad_up_part], axis=1).astype(jnp.bfloat16)
    grad_gateup = contract(normed_ffn, grad_gate_up, 0, 0)
    grad_normed_ffn = contract(grad_gate_up, gateup_weight, 1, 1)
    scale_ffn = 1.0 + mod_ffn[:, model_width : 2 * model_width]
    grad_shift_ffn = jnp.sum(grad_normed_ffn, axis=0, keepdims=True)
    grad_scale_ffn = jnp.sum(grad_normed_ffn * ffn_hat * norm_ffn, axis=0, keepdims=True)
    grad_norm_ffn = jnp.sum(grad_normed_ffn * ffn_hat * scale_ffn, axis=0)
    grad_after = grad_out + normed_back(grad_normed_ffn * norm_ffn * scale_ffn, ffn_hat, ffn_inv)
    grad_branch_attn = (mod_attn[:, 2 * model_width :] * row_live * grad_after).astype(jnp.bfloat16)
    grad_gate_attn = jnp.sum(row_live * branch_attn * grad_after, axis=0, keepdims=True)
    grad_outw = contract(attn_mixed, grad_branch_attn, 0, 0)
    grad_mixed = (
        contract(grad_branch_attn, out_weight, 1, 1)
        .astype(jnp.bfloat16)
        .reshape(length, head_count, head_size)
    )
    grad_probs = jnp.einsum(
        "ihd,jhd->hij", grad_mixed, value_heads, preferred_element_type=jnp.float32
    )
    grad_values = jnp.einsum(
        "hij,ihd->jhd", probs_low, grad_mixed, preferred_element_type=jnp.float32
    )
    grad_scores = (
        attn_probs * (grad_probs - jnp.sum(attn_probs * grad_probs, axis=-1, keepdims=True))
    ).astype(jnp.bfloat16)
    grad_query = (
        jnp.einsum("hij,jhd->ihd", grad_scores, key_heads, preferred_element_type=jnp.float32)
        * score_scale
    )
    grad_keys = (
        jnp.einsum("hij,ihd->jhd", grad_scores, query_heads, preferred_element_type=jnp.float32)
        * score_scale
    )
    grad_projected = jnp.concatenate(
        [
            grad_query.reshape(length, model_width),
            grad_keys.reshape(length, model_width),
            grad_values.reshape(length, model_width),
        ],
        axis=1,
    ).astype(jnp.bfloat16)
    grad_qkv = contract(normed_attn, grad_projected, 0, 0)
    grad_normed_attn = contract(grad_projected, qkv_weight, 1, 1)
    scale_attn = 1.0 + mod_attn[:, model_width : 2 * model_width]
    grad_shift_attn = jnp.sum(grad_normed_attn, axis=0, keepdims=True)
    grad_scale_attn = jnp.sum(grad_normed_attn * attn_hat * norm_attn, axis=0, keepdims=True)
    grad_norm_attn = jnp.sum(grad_normed_attn * attn_hat * scale_attn, axis=0)
    grad_act = grad_after + normed_back(
        grad_normed_attn * norm_attn * scale_attn, attn_hat, attn_inv
    )
    grad_pairw = jnp.einsum("ijc,hij->ch", pair_in, grad_scores, preferred_element_type=jnp.float32)
    grad_pair_in = jnp.einsum(
        "hij,ch->ijc", grad_scores, pair_weight, preferred_element_type=jnp.float32
    )
    grad_pair_gain = jnp.sum(grad_pair_in * pair_hat, axis=(0, 1))
    grad_pair = normed_back(grad_pair_in * pair_gain, pair_hat, pair_inv).astype(jnp.bfloat16)
    grad_mod_attn = jnp.concatenate([grad_shift_attn, grad_scale_attn, grad_gate_attn], axis=1)
    grad_mod_ffn = jnp.concatenate([grad_shift_ffn, grad_scale_ffn, grad_gate_ffn], axis=1)
    cond_float = cond_act.astype(jnp.float32)
    cond_column = cond_float.reshape(-1, 1)
    grad_cond_attn = cond_column * grad_mod_attn
    grad_cond_ffn = cond_column * grad_mod_ffn
    grad_cond_act = jnp.einsum(
        "ak,bk->ab", grad_mod_attn, cond_attn, precision=highest
    ) + jnp.einsum("ak,bk->ab", grad_mod_ffn, cond_ffn, precision=highest)
    grad_cond = grad_cond_act * silu_slope(cond_raw)
    grad_cath = cath_hot.astype(jnp.float32).reshape(-1, 1) * grad_cond
    grad_time = time_hot.astype(jnp.float32).reshape(-1, 1) * grad_cond
    grads = (
        grad_cath,
        grad_time,
        grad_cond_attn,
        grad_cond_ffn,
        grad_norm_attn,
        grad_norm_ffn,
        grad_pair_gain,
        grad_qkv,
        grad_outw,
        grad_pairw,
        grad_gateup,
        grad_down,
    )
    factors = (cond_float, grad_mod_attn, grad_mod_ffn, grad_cond)
    return (grad_act, grad_pair, grads, factors)


def shards(
    activations,
    pair_repr,
    cotangent,
    buckets,
    pad_mask,
    cath_ids,
    time_bins,
    cath_table,
    time_table,
    cond_attn,
    cond_ffn,
    norm_attn,
    norm_ffn,
    pair_gain,
    qkv_weight,
    out_weight,
    pair_weight,
    gateup_weight,
    down_weight,
):
    micro_count = activations.shape[0]
    length = activations.shape[2]
    positions = lax.broadcasted_iota(jnp.int32, (length,), 0)
    outputs = []
    grad_acts = []
    grad_pairs = []
    totals = ()
    for micro_index in range(micro_count):
        forward_weights = (
            lax.all_gather(cath_table, "fsdp", axis=1, tiled=True),
            lax.all_gather(time_table, "fsdp", axis=1, tiled=True),
            lax.all_gather(cond_attn, "fsdp", axis=0, tiled=True),
            lax.all_gather(cond_ffn, "fsdp", axis=0, tiled=True),
            lax.all_gather(norm_attn, "fsdp", axis=0, tiled=True),
            lax.all_gather(norm_ffn, "fsdp", axis=0, tiled=True),
            lax.all_gather(pair_gain, "fsdp", axis=0, tiled=True),
            lax.all_gather(qkv_weight, "fsdp", axis=0, tiled=True),
            lax.all_gather(out_weight, "fsdp", axis=0, tiled=True),
            lax.all_gather(pair_weight, "fsdp", axis=0, tiled=True),
            lax.all_gather(gateup_weight, "fsdp", axis=0, tiled=True),
            lax.all_gather(down_weight, "fsdp", axis=0, tiled=True),
        )
        chain_act = activations[micro_index, 0].astype(jnp.float32)
        live_keys = (positions < buckets[micro_index, 0]) & (
            (pad_mask[micro_index, 0] == 1) | (positions == 0)
        )
        output, saved = layer_forward(
            forward_weights,
            chain_act,
            pair_repr[micro_index, 0],
            live_keys,
            cath_ids[micro_index, 0],
            time_bins[micro_index, 0],
        )
        outputs.append(output.astype(jnp.bfloat16))
        grad_act, grad_pair, grads, factors = layer_backward(
            forward_weights, saved, cotangent[micro_index, 0].astype(jnp.float32)
        )
        grad_acts.append(grad_act.astype(jnp.bfloat16))
        grad_pairs.append(grad_pair)
        owned = (
            lax.psum_scatter(
                grads[0].astype(jnp.bfloat16), "fsdp", scatter_dimension=1, tiled=True
            ).astype(jnp.float32),
            lax.psum_scatter(
                grads[1].astype(jnp.bfloat16), "fsdp", scatter_dimension=1, tiled=True
            ).astype(jnp.float32),
            lax.psum_scatter(
                grads[2].astype(jnp.bfloat16), "fsdp", scatter_dimension=0, tiled=True
            ).astype(jnp.float32),
            lax.psum_scatter(
                grads[3].astype(jnp.bfloat16), "fsdp", scatter_dimension=0, tiled=True
            ).astype(jnp.float32),
            lax.psum_scatter(
                grads[4].astype(jnp.bfloat16), "fsdp", scatter_dimension=0, tiled=True
            ).astype(jnp.float32),
            lax.psum_scatter(
                grads[5].astype(jnp.bfloat16), "fsdp", scatter_dimension=0, tiled=True
            ).astype(jnp.float32),
            lax.psum_scatter(
                grads[6].astype(jnp.bfloat16), "fsdp", scatter_dimension=0, tiled=True
            ).astype(jnp.float32),
            lax.psum_scatter(
                grads[7].astype(jnp.bfloat16), "fsdp", scatter_dimension=0, tiled=True
            ).astype(jnp.float32),
            lax.psum_scatter(
                grads[8].astype(jnp.bfloat16), "fsdp", scatter_dimension=0, tiled=True
            ).astype(jnp.float32),
            lax.psum_scatter(
                grads[9].astype(jnp.bfloat16), "fsdp", scatter_dimension=0, tiled=True
            ).astype(jnp.float32),
            lax.psum_scatter(
                grads[10].astype(jnp.bfloat16), "fsdp", scatter_dimension=0, tiled=True
            ).astype(jnp.float32),
            lax.psum_scatter(
                grads[11].astype(jnp.bfloat16), "fsdp", scatter_dimension=0, tiled=True
            ).astype(jnp.float32),
        )
        owned = (
            lax.psum(owned[0].astype(jnp.bfloat16), "dp").astype(jnp.float32),
            lax.psum(owned[1].astype(jnp.bfloat16), "dp").astype(jnp.float32),
            lax.psum(owned[2].astype(jnp.bfloat16), "dp").astype(jnp.float32),
            lax.psum(owned[3].astype(jnp.bfloat16), "dp").astype(jnp.float32),
            lax.psum(owned[4].astype(jnp.bfloat16), "dp").astype(jnp.float32),
            lax.psum(owned[5].astype(jnp.bfloat16), "dp").astype(jnp.float32),
            lax.psum(owned[6].astype(jnp.bfloat16), "dp").astype(jnp.float32),
            lax.psum(owned[7].astype(jnp.bfloat16), "dp").astype(jnp.float32),
            lax.psum(owned[8].astype(jnp.bfloat16), "dp").astype(jnp.float32),
            lax.psum(owned[9].astype(jnp.bfloat16), "dp").astype(jnp.float32),
            lax.psum(owned[10].astype(jnp.bfloat16), "dp").astype(jnp.float32),
            lax.psum(owned[11].astype(jnp.bfloat16), "dp").astype(jnp.float32),
        )
        if micro_index == 0:
            totals = tuple(owned)
        else:
            totals = tuple((earlier + current for earlier, current in zip(totals, owned)))
    return (
        jnp.stack(outputs)[:, None],
        jnp.stack(grad_acts)[:, None],
        jnp.stack(grad_pairs)[:, None],
        totals[0],
        totals[1],
        totals[2],
        totals[3],
        totals[4],
        totals[5],
        totals[6],
        totals[7],
        totals[8],
        totals[9],
        totals[10],
        totals[11],
    )


def solution(mesh):
    in_specs = (
        P(None, ("dp", "fsdp"), None, None),
        P(None, ("dp", "fsdp"), None, None, None),
        P(None, ("dp", "fsdp"), None, None),
        P(None, ("dp", "fsdp")),
        P(None, ("dp", "fsdp"), None),
        P(None, ("dp", "fsdp")),
        P(None, ("dp", "fsdp")),
        P(None, "fsdp"),
        P(None, "fsdp"),
        P("fsdp", None),
        P("fsdp", None),
        P("fsdp"),
        P("fsdp"),
        P("fsdp"),
        P("fsdp", None),
        P("fsdp", None),
        P("fsdp", None),
        P("fsdp", None),
        P("fsdp", None),
    )
    out_specs = (
        P(None, ("dp", "fsdp"), None, None),
        P(None, ("dp", "fsdp"), None, None),
        P(None, ("dp", "fsdp"), None, None, None),
        P(None, "fsdp"),
        P(None, "fsdp"),
        P("fsdp", None),
        P("fsdp", None),
        P("fsdp"),
        P("fsdp"),
        P("fsdp"),
        P("fsdp", None),
        P("fsdp", None),
        P("fsdp", None),
        P("fsdp", None),
        P("fsdp", None),
    )
    return jax.shard_map(shards, mesh=mesh, in_specs=in_specs, out_specs=out_specs, check_vma=False)
```

profile of v0, /device:TPU:0, one launch (start us, length us, event | category | flops | bytes accessed | tf_op | source)
XLA Modules:
  0.0 1866.2 jit_solution(4064559085240703334)
XLA Ops:
  25.7 35.7 %all-reduce.10 = (bf16[768]{0:T(1024)(128)(2,1)S(1)}, bf16[256]{0:T(256)(128)(2,1)S(1)}, bf16[768]{0:T(1024)(128)(2,1)S(1)}) all-reduce(bf16[768]{0:T(1024)(128)(2,1)S(1)} %dynamic-update-slice, bf16[256]{0:T(256)(128)(2,1)S(1)} %dynamic-update-slice.1, bf16[768]{0:T(1024)(128)(2,1)S(1)} %dynamic-update-slice.2), channel_id=1, replica_groups=mesh['dp'=2,'fsdp'=16] {'fsdp'}, use_global_device_ids=true, to_apply=%add | all-reduce | flops 1792 | bytes 7168
  146.5 44.1 %all-gather.15.cloned.1.call-done = bf16[768,2304]{1,0:T(8,128)(2,1)} async-done(((bf16[48,2304]{1,0:T(8,128)(2,1)}), bf16[768,2304]{1,0:T(8,128)(2,1)}) %all-gather.15.cloned.1.call-update) | async-done | bytes 3538960 | tf_op jit(solution)/shard_map/all_gather | solution.py:324
  208.4 30.5 %all-gather.19.cloned.1.call-done = bf16[768,2304]{1,0:T(8,128)(2,1)} async-done(((bf16[48,2304]{1,0:T(8,128)(2,1)}), bf16[768,2304]{1,0:T(8,128)(2,1)}) %all-gather.19.cloned.1.call-update) | async-done | bytes 3538960 | tf_op jit(solution)/shard_map/all_gather | solution.py:320
  284.9 76.3 %all-gather.21.cloned.1.call-done = bf16[768,6144]{1,0:T(8,128)(2,1)} async-done(((bf16[48,6144]{1,0:T(8,128)(2,1)}), bf16[768,6144]{1,0:T(8,128)(2,1)}) %all-gather.21.cloned.1.call-update) | async-done | bytes 9437200 | tf_op jit(solution)/shard_map/all_gather | solution.py:327
  367.6 47.4 %all-gather.23.cloned.1.call-done = bf16[3072,768]{1,0:T(8,128)(2,1)} async-done(((bf16[192,768]{1,0:T(8,128)(2,1)}), bf16[3072,768]{1,0:T(8,128)(2,1)}) %all-gather.23.cloned.1.call-update) | async-done | bytes 4718608 | tf_op jit(solution)/shard_map/all_gather | solution.py:328
  548.4 30.9 %fusion.28 = (bf16[256]{0:T(256)(128)(2,1)S(1)}, f32[128,128]{1,0:T(8,128)S(1)}, f32[128,128]{1,0:T(8,128)S(1)}, bf16[256]{0:T(256)(128)(2,1)S(1)}, f32[128,128]...) fusion(f32[128,128]{1,0:T(8,128)S(1)} %copy-done.78, f32[128,128]{1,0:T(8,128)S(1)} %copy-done.60, ...), kind=kOutput, calls=%fused_computation.32 | convolution fusion | flops 176094720 | bytes 51257344 | tf_op jit(solution)/shard_map/hij,ch->ijc/dot_general | solution.py:252
  604.4 31.3 %reduce-scatter.23.cloned.1.call-done = bf16[1000,48]{0,1:T(8,128)(2,1)} async-done(((bf16[1000,768]{0,1:T(8,128)(2,1)}), bf16[1000,48]{0,1:T(8,128)(2,1)}) %reduce-scatter.23.cloned.1.call-update) | async-done | bytes 96016 | tf_op jit(solution)/shard_map/reduce_scatter | solution.py:352
  635.7 62.6 %reduce-scatter.25.cloned.1.call-done = bf16[1000,48]{0,1:T(8,128)(2,1)} async-done(((bf16[1000,768]{0,1:T(8,128)(2,1)}), bf16[1000,48]{0,1:T(8,128)(2,1)}) %reduce-scatter.25.cloned.1.call-update) | async-done | bytes 96016 | tf_op jit(solution)/shard_map/reduce_scatter | solution.py:352
  698.3 62.2 %reduce-scatter.19.cloned.1.call-done = bf16[1024,48]{0,1:T(8,128)(2,1)} async-done(((bf16[1024,768]{0,1:T(8,128)(2,1)}), bf16[1024,48]{0,1:T(8,128)(2,1)}) %reduce-scatter.19.cloned.1.call-update) | async-done | bytes 98320 | tf_op jit(solution)/shard_map/reduce_scatter | solution.py:349
  760.5 62.5 %reduce-scatter.21.cloned.1.call-done = bf16[1024,48]{0,1:T(8,128)(2,1)} async-done(((bf16[1024,768]{0,1:T(8,128)(2,1)}), bf16[1024,48]{0,1:T(8,128)(2,1)}) %reduce-scatter.21.cloned.1.call-update) | async-done | bytes 98320 | tf_op jit(solution)/shard_map/reduce_scatter | solution.py:349
  823.0 70.8 %reduce-scatter.37.cloned.1.call-done = bf16[48,2304]{1,0:T(8,128)(2,1)} async-done(((bf16[768,2304]{1,0:T(8,128)(2,1)}), bf16[48,2304]{1,0:T(8,128)(2,1)}) %reduce-scatter.37.cloned.1.call-update) | async-done | bytes 221200 | tf_op jit(solution)/shard_map/reduce_scatter | solution.py:370
  893.7 70.6 %reduce-scatter.35.cloned.1.call-done = bf16[48,2304]{1,0:T(8,128)(2,1)} async-done(((bf16[768,2304]{1,0:T(8,128)(2,1)}), bf16[48,2304]{1,0:T(8,128)(2,1)}) %reduce-scatter.35.cloned.1.call-update) | async-done | bytes 221200 | tf_op jit(solution)/shard_map/reduce_scatter | solution.py:370
  964.4 70.6 %reduce-scatter.31.cloned.1.call-done = bf16[48,2304]{1,0:T(8,128)(2,1)} async-done(((bf16[768,2304]{1,0:T(8,128)(2,1)}), bf16[48,2304]{1,0:T(8,128)(2,1)}) %reduce-scatter.31.cloned.1.call-update) | async-done | bytes 221200 | tf_op jit(solution)/shard_map/reduce_scatter | solution.py:358
  1035.0 70.6 %reduce-scatter.27.cloned.1.call-done = bf16[48,2304]{1,0:T(8,128)(2,1)} async-done(((bf16[768,2304]{1,0:T(8,128)(2,1)}), bf16[48,2304]{1,0:T(8,128)(2,1)}) %reduce-scatter.27.cloned.1.call-update) | async-done | bytes 221200 | tf_op jit(solution)/shard_map/reduce_scatter | solution.py:355
  1105.6 70.8 %reduce-scatter.33.cloned.1.call-done = bf16[48,2304]{1,0:T(8,128)(2,1)} async-done(((bf16[768,2304]{1,0:T(8,128)(2,1)}), bf16[48,2304]{1,0:T(8,128)(2,1)}) %reduce-scatter.33.cloned.1.call-update) | async-done | bytes 221200 | tf_op jit(solution)/shard_map/reduce_scatter | solution.py:358
  1176.4 70.6 %reduce-scatter.29.cloned.1.call-done = bf16[48,2304]{1,0:T(8,128)(2,1)} async-done(((bf16[768,2304]{1,0:T(8,128)(2,1)}), bf16[48,2304]{1,0:T(8,128)(2,1)}) %reduce-scatter.29.cloned.1.call-update) | async-done | bytes 221200 | tf_op jit(solution)/shard_map/reduce_scatter | solution.py:355
  1247.0 78.2 %reduce-scatter.51.cloned.1.call-done = bf16[192,768]{1,0:T(8,128)(2,1)} async-done(((bf16[3072,768]{1,0:T(8,128)(2,1)}), bf16[192,768]{1,0:T(8,128)(2,1)}) %reduce-scatter.51.cloned.1.call-update) | async-done | bytes 294928 | tf_op jit(solution)/shard_map/reduce_scatter | solution.py:382
  1325.2 79.0 %reduce-scatter.53.cloned.1.call-done = bf16[192,768]{1,0:T(8,128)(2,1)} async-done(((bf16[3072,768]{1,0:T(8,128)(2,1)}), bf16[192,768]{1,0:T(8,128)(2,1)}) %reduce-scatter.53.cloned.1.call-update) | async-done | bytes 294928 | tf_op jit(solution)/shard_map/reduce_scatter | solution.py:382
  1404.3 114.5 %reduce-scatter.49.cloned.1.call-done = bf16[48,6144]{1,0:T(8,128)(2,1)} async-done(((bf16[768,6144]{1,0:T(8,128)(2,1)}), bf16[48,6144]{1,0:T(8,128)(2,1)}) %reduce-scatter.49.cloned.1.call-update) | async-done | bytes 589840 | tf_op jit(solution)/shard_map/reduce_scatter | solution.py:379
  1518.8 115.7 %reduce-scatter.47.cloned.1.call-done = bf16[48,6144]{1,0:T(8,128)(2,1)} async-done(((bf16[768,6144]{1,0:T(8,128)(2,1)}), bf16[48,6144]{1,0:T(8,128)(2,1)}) %reduce-scatter.47.cloned.1.call-update) | async-done | bytes 589840 | tf_op jit(solution)/shard_map/reduce_scatter | solution.py:379
  1634.6 23.5 %fusion.31 = (bf16[1,128,128,256]{3,2,1,0:T(8,128)(2,1)}, bf16[1,128,128,256]{3,2,1,0:T(8,128)(2,1)}) fusion(f32[128,128,256]{2,1,0:T(8,128)} %copy-done.1, f32[128,128]{1,0:T(8,128)S(1)} %broadcast_multiply_fusion.2, f32[128,128]{1,0:T(8,128)S(1)} %broadcast_multiply_fusion.3, f32[256]{0:T(256)S(1)} %copy-done.158, f32[128,128]{1,0:T(8,128)S(1)} %copy-done.76, ...), kind=kLoop, calls=%fused_computation.40 | loop fusion | flops 75497472 | bytes 67634176 | tf_op jit(solution)/shard_map/stack | solution.py:407
  1658.2 33.2 %all-reduce.9 = (bf16[768]{0:T(1024)(128)(2,1)S(1)}, bf16[768]{0:T(1024)(128)(2,1)S(1)}, bf16[768]{0:T(1024)(128)(2,1)S(1)}, bf16[768]{0:T(1024)(128)(2,1)S(1)},...) all-reduce(bf16[768]{0:T(1024)(128)(2,1)S(1)} %copy-done.156, ...), channel_id=11, replica_groups=mesh['dp'=2,'fsdp'=16] {'fsdp'}, use_global_device_ids=true, to_apply=%region_62.63.clone | all-reduce | flops 3584 | bytes 14336
  1707.7 37.4 %reduce-scatter.45.cloned.1.call-done = bf16[16,12]{1,0:T(8,128)(2,1)} async-done(((bf16[256,12]{1,0:T(8,128)(2,1)}), bf16[16,12]{1,0:T(8,128)(2,1)}) %reduce-scatter.45.cloned.1.call-update) | async-done | bytes 400 | tf_op jit(solution)/shard_map/reduce_scatter | solution.py:376
  1756.0 90.3 %all-reduce.15.cloned.1.call-done = (bf16[1024,48]{0,1:T(8,128)(2,1)}, bf16[1024,48]{0,1:T(8,128)(2,1)}, bf16[1000,48]{0,1:T(8,128)(2,1)}, bf16[1000,48]{0,1:T(8...) async-done(((bf16[1024,48]{0,1:T(8,128)(2,1)}, ...) | async-done | bytes 3632656 | tf_op jit(solution)/shard_map/psum | solution.py:387
  (583 shorter events, 367.1 us)
Async XLA Ops:
  9.4 181.2 %all-gather.15.cloned.1.call-start = ((), (), s32[]{:S(2)}) async-start(), calls=%async_computation.21 | async-start | bytes 3760128 | tf_op jit(solution)/shard_map/all_gather | solution.py:324
  10.0 228.9 %all-gather.19.cloned.1.call-start = ((), (), s32[]{:S(2)}) async-start(), calls=%async_computation.23 | async-start | bytes 3760128 | tf_op jit(solution)/shard_map/all_gather | solution.py:320
  10.6 267.9 %all-gather.17.cloned.1.call-start = ((), (), s32[]{:S(2)}) async-start(), calls=%async_computation.22 | async-start | bytes 1253376 | tf_op jit(solution)/shard_map/all_gather | solution.py:325
  11.1 350.0 %all-gather.21.cloned.1.call-start = ((), (), s32[]{:S(2)}) async-start(), calls=%async_computation.24 | async-start | bytes 10027008 | tf_op jit(solution)/shard_map/all_gather | solution.py:327
  11.9 403.1 %all-gather.23.cloned.1.call-start = ((), (), s32[]{:S(2)}) async-start(), calls=%async_computation.25 | async-start | bytes 5013504 | tf_op jit(solution)/shard_map/all_gather | solution.py:328
  12.6 591.7 %reduce-scatter.41.cloned.1.call-start = ((), (), s32[]{:S(2)}) async-start(), calls=%async_computation.37 | async-start | bytes 1253376 | tf_op jit(solution)/shard_map/reduce_scatter | solution.py:373
  456.2 148.2 %reduce-scatter.39.cloned.1.call-start = ((), (), s32[]{:S(2)}) async-start(), calls=%async_computation.36 | async-start | bytes 1253376 | tf_op jit(solution)/shard_map/reduce_scatter | solution.py:373
  466.6 169.2 %reduce-scatter.23.cloned.1.call-start = ((), (), s32[]{:S(2)}) async-start(), calls=%async_computation.28 | async-start | bytes 1671168 | tf_op jit(solution)/shard_map/reduce_scatter | solution.py:352
  481.6 216.7 %reduce-scatter.25.cloned.1.call-start = ((), (), s32[]{:S(2)}) async-start(), calls=%async_computation.29 | async-start | bytes 1671168 | tf_op jit(solution)/shard_map/reduce_scatter | solution.py:352
  495.9 264.6 %reduce-scatter.19.cloned.1.call-start = ((), (), s32[]{:S(2)}) async-start(), calls=%async_computation.26 | async-start | bytes 1671168 | tf_op jit(solution)/shard_map/reduce_scatter | solution.py:349
  498.8 324.2 %reduce-scatter.21.cloned.1.call-start = ((), (), s32[]{:S(2)}) async-start(), calls=%async_computation.27 | async-start | bytes 1671168 | tf_op jit(solution)/shard_map/reduce_scatter | solution.py:349
  501.0 392.8 %reduce-scatter.37.cloned.1.call-start = ((), (), s32[]{:S(2)}) async-start(), calls=%async_computation.35 | async-start | bytes 3760128 | tf_op jit(solution)/shard_map/reduce_scatter | solution.py:370
  504.3 460.1 %reduce-scatter.35.cloned.1.call-start = ((), (), s32[]{:S(2)}) async-start(), calls=%async_computation.34 | async-start | bytes 3760128 | tf_op jit(solution)/shard_map/reduce_scatter | solution.py:370
  507.6 527.4 %reduce-scatter.31.cloned.1.call-start = ((), (), s32[]{:S(2)}) async-start(), calls=%async_computation.32 | async-start | bytes 3760128 | tf_op jit(solution)/shard_map/reduce_scatter | solution.py:358
  513.0 592.6 %reduce-scatter.27.cloned.1.call-start = ((), (), s32[]{:S(2)}) async-start(), calls=%async_computation.30 | async-start | bytes 3760128 | tf_op jit(solution)/shard_map/reduce_scatter | solution.py:355
  513.6 662.8 %reduce-scatter.33.cloned.1.call-start = ((), (), s32[]{:S(2)}) async-start(), calls=%async_computation.33 | async-start | bytes 3760128 | tf_op jit(solution)/shard_map/reduce_scatter | solution.py:358
  518.9 728.1 %reduce-scatter.29.cloned.1.call-start = ((), (), s32[]{:S(2)}) async-start(), calls=%async_computation.31 | async-start | bytes 3760128 | tf_op jit(solution)/shard_map/reduce_scatter | solution.py:355
  519.5 805.7 %reduce-scatter.51.cloned.1.call-start = ((), (), s32[]{:S(2)}) async-start(), calls=%async_computation.42 | async-start | bytes 5013504 | tf_op jit(solution)/shard_map/reduce_scatter | solution.py:382
  524.2 880.1 %reduce-scatter.53.cloned.1.call-start = ((), (), s32[]{:S(2)}) async-start(), calls=%async_computation.43 | async-start | bytes 5013504 | tf_op jit(solution)/shard_map/reduce_scatter | solution.py:382
  529.4 989.3 %reduce-scatter.49.cloned.1.call-start = ((), (), s32[]{:S(2)}) async-start(), calls=%async_computation.41 | async-start | bytes 10027008 | tf_op jit(solution)/shard_map/reduce_scatter | solution.py:379
  536.3 1098.1 %reduce-scatter.47.cloned.1.call-start = ((), (), s32[]{:S(2)}) async-start(), calls=%async_computation.40 | async-start | bytes 10027008 | tf_op jit(solution)/shard_map/reduce_scatter | solution.py:379
  543.2 1164.5 %reduce-scatter.43.cloned.1.call-start = ((), (), s32[]{:S(2)}) async-start(), calls=%async_computation.38 | async-start | bytes 69632 | tf_op jit(solution)/shard_map/reduce_scatter | solution.py:376
  603.7 1141.4 %reduce-scatter.45.cloned.1.call-start = ((), (), s32[]{:S(2)}) async-start(), calls=%async_computation.39 | async-start | bytes 69632 | tf_op jit(solution)/shard_map/reduce_scatter | solution.py:376
  604.3 1242.0 %all-reduce.15.cloned.1.call-start = ((), (), s32[]{:S(2)}) async-start(), calls=%async_computation.44 | async-start | bytes 7274496 | tf_op jit(solution)/shard_map/psum | solution.py:387
  (172 other events, 2026.1 us)
Sparse Core Ops, SparseCore 0:
  96.1 45.9 all-gather.12
  144.3 46.1 all-gather.14
  192.7 46.1 all-gather.18
  280.7 80.4 all-gather.20
  363.4 51.5 all-gather.22
  456.3 56.6 reduce-scatter.40
  516.4 57.0 reduce-scatter.38
  577.2 58.4 reduce-scatter.22
  639.7 58.5 reduce-scatter.24
  702.0 58.4 reduce-scatter.18
  764.4 58.4 reduce-scatter.20
  826.7 67.0 reduce-scatter.36
  897.5 66.8 reduce-scatter.34
  968.1 66.8 reduce-scatter.30
  1038.7 66.8 reduce-scatter.26
  1109.5 66.8 reduce-scatter.32
  1180.1 66.8 reduce-scatter.28
  1250.9 74.3 reduce-scatter.50
  1329.6 74.6 reduce-scatter.52
  1408.4 110.3 reduce-scatter.48
  1523.3 111.1 reduce-scatter.46
  1638.4 51.6 reduce-scatter.42
  1694.2 50.8 reduce-scatter.44
  1748.2 98.0 all-reduce.14
  (3 shorter events, 118.4 us)
where the time goes:
time: 1870 us
  waiting for transfers between devices  1400 us (75%)
  matrix products  193 us (10%)
  other arithmetic  114 us (6%)
  blocking collectives  95.4 us (5%)
  local copies, waits for them, and re-layouts  46 us (2%)
  between operations  19.8 us (1%)
    reduce_scatter x2, waiting for transfers between devices, shards(): lax.psum_scatter(grads[10].astype(jnp.bfloat16), 'fsdp', scatter_dimensio...  230 us
    reduce_scatter x2, waiting for transfers between devices, shards(): lax.psum_scatter(grads[11].astype(jnp.bfloat16), 'fsdp', scatter_dimensio...  157 us
    reduce_scatter x2, waiting for transfers between devices, shards(): lax.psum_scatter(grads[7].astype(jnp.bfloat16), 'fsdp', scatter_dimension...  141 us
    reduce_scatter x2, waiting for transfers between devices, shards(): lax.psum_scatter(grads[3].astype(jnp.bfloat16), 'fsdp', scatter_dimension...  141 us
    reduce_scatter x2, waiting for transfers between devices, shards(): lax.psum_scatter(grads[2].astype(jnp.bfloat16), 'fsdp', scatter_dimension...  141 us
    reduce_scatter x2, waiting for transfers between devices, shards(): lax.psum_scatter(grads[0].astype(jnp.bfloat16), 'fsdp', scatter_dimension...  125 us
    reduce_scatter x2, waiting for transfers between devices, shards(): lax.psum_scatter(grads[1].astype(jnp.bfloat16), 'fsdp', scatter_dimension...  93.9 us
    psum x1, waiting for transfers between devices, shards(): lax.psum(owned[0].astype(jnp.bfloat16), 'dp').astype(jnp.float32)  90.3 us
  transfers between devices with their start and end apart: 27, of which 22 were waited for; matrix products, arithmetic and copies ran while one was open for 15% of the time, Pallas kernels for 0%

commit v1 on v0

v1 whole, which is shorter than its diff:
```python
import math
import jax
import jax.numpy as jnp
from jax import lax
from jax.experimental import pallas as pl
from jax.experimental.pallas import tpu as pltpu
from jax.sharding import PartitionSpec as P

F32 = jnp.float32
BF16 = jnp.bfloat16
EPS = 1e-05
SLOTS = 16
EVERY = ("dp", "fsdp")
VMEM_BYTES = 48 * 1024 * 1024


def dot(a, b, a_dim, b_dim):
    return lax.dot_general(a, b, (((a_dim,), (b_dim,)), ((), ())), preferred_element_type=F32)


def pair_forward_kernel(pair_ref, center_ref, weight_ref, square_ref, out_ref):
    rows, length, channels = pair_ref.shape[1:]
    group = length // SLOTS
    slot = lax.broadcasted_iota(jnp.int32, (group, SLOTS, length), 1)
    for start in range(0, rows, group):
        block = pair_ref[0, start : start + group].reshape(group * length, channels)
        centered = dot(block, center_ref[...], 1, 0)
        low = centered.astype(BF16)
        square = (centered * centered).astype(BF16)
        raw = dot(low, weight_ref[...], 1, 0) + dot(square, square_ref[...], 1, 0)
        packed = raw[:length]
        for k in range(1, group):
            packed = packed + pltpu.roll(raw[k * length : (k + 1) * length], SLOTS * k, 1)
        turned = packed.T.reshape(group, SLOTS, length)
        inverse = lax.rsqrt(turned[:, SLOTS - 1 :, :] + EPS)
        out_ref[0, start : start + group] = jnp.where(slot == SLOTS - 1, inverse, turned * inverse)


def pair_forward(pair, center, weight, square):
    count, length, _, channels = pair.shape
    rows = 16
    return pl.pallas_call(
        pair_forward_kernel,
        grid=(count, length // rows),
        in_specs=[
            pl.BlockSpec((1, rows, length, channels), lambda n, i: (n, i, 0, 0)),
            pl.BlockSpec(center.shape, lambda n, i: (0, 0)),
            pl.BlockSpec(weight.shape, lambda n, i: (0, 0)),
            pl.BlockSpec(square.shape, lambda n, i: (0, 0)),
        ],
        out_specs=pl.BlockSpec((1, rows, SLOTS, length), lambda n, i: (n, i, 0, 0)),
        out_shape=jax.ShapeDtypeStruct((count, length, SLOTS, length), F32),
        compiler_params=pltpu.CompilerParams(vmem_limit_bytes=VMEM_BYTES),
        cost_estimate=pl.CostEstimate(
            flops=2 * pair.size * 3 * 256, bytes_accessed=2 * pair.size, transcendentals=0
        ),
        name="pair_forward",
    )(pair, center, weight, square)


def pair_backward_kernel(heads, pair_ref, grad_ref, stat_ref, center_ref, spread_ref, out_ref, sum_ref):
    rows, length, channels = pair_ref.shape[1:]
    group = length // SLOTS

    @pl.when((pl.program_id(0) == 0) & (pl.program_id(1) == 0))
    def _():
        sum_ref[...] = jnp.zeros_like(sum_ref)

    slot = lax.broadcasted_iota(jnp.int32, (group, SLOTS, length), 1)
    lane_slot = lax.broadcasted_iota(jnp.int32, (length, length), 1) // SLOTS
    total = jnp.zeros(sum_ref.shape, F32)
    for start in range(0, rows, group):
        block = pair_ref[0, start : start + group].reshape(group * length, channels)
        centered = dot(block, center_ref[...], 1, 0)
        low = centered.astype(BF16)
        grads = jnp.where(slot < heads, grad_ref[0, start : start + group], 0.0)
        stats = stat_ref[0, start : start + group]
        inverse = stats[:, SLOTS - 1 :, :]
        inner = jnp.sum(jnp.where(slot < heads, grads * stats, 0.0), axis=1, keepdims=True)
        slope = inner * inverse * inverse * (-1.0 / channels)
        slope_high = slope.astype(BF16).astype(F32)
        left = jnp.where(slot < heads, grads * inverse, 0.0)
        left = jnp.where(slot == heads, slope_high, left)
        left = jnp.where(slot == heads + 1, slope - slope_high, left)
        left = left.reshape(group * SLOTS, length)
        left_low = left.astype(BF16)
        turned = left.T.astype(BF16)
        for k in range(group):
            part = jnp.where(lane_slot == k, turned, jnp.zeros_like(turned))
            spread = dot(part, spread_ref[...], 1, 0)
            here = slice(k * length, (k + 1) * length)
            out_ref[0, start + k] = (spread[:, :channels] + centered[here] * spread[:, channels:]).astype(BF16)
            total = total + dot(left_low[k * SLOTS : (k + 1) * SLOTS], low[here], 1, 0)
    sum_ref[...] += total


def pair_backward(heads, pair, grads, stats, center, spread):
    count, length, _, channels = pair.shape
    rows = 16
    small = pl.BlockSpec((1, rows, SLOTS, length), lambda n, i: (n, i, 0, 0))
    large = pl.BlockSpec((1, rows, length, channels), lambda n, i: (n, i, 0, 0))
    return pl.pallas_call(
        lambda *refs: pair_backward_kernel(heads, *refs),
        grid=(count, length // rows),
        in_specs=[
            large,
            small,
            small,
            pl.BlockSpec(center.shape, lambda n, i: (0, 0)),
            pl.BlockSpec(spread.shape, lambda n, i: (0, 0)),
        ],
        out_specs=[large, pl.BlockSpec((SLOTS, channels), lambda n, i: (0, 0))],
        out_shape=[
            jax.ShapeDtypeStruct(pair.shape, BF16),
            jax.ShapeDtypeStruct((SLOTS, channels), F32),
        ],
        compiler_params=pltpu.CompilerParams(vmem_limit_bytes=VMEM_BYTES),
        cost_estimate=pl.CostEstimate(
            flops=2 * pair.size * 4 * 256, bytes_accessed=4 * pair.size, transcendentals=0
        ),
        name="pair_backward",
    )(pair, grads, stats, center, spread)


def split_pair(values, low_half):
    zero = jnp.zeros_like(values)
    return jnp.concatenate([jnp.where(low_half, values, zero), jnp.where(low_half, zero, values)], axis=0)


def attention_forward_kernel(scale, qkv_ref, stat_ref, live_ref, probs_ref, mixed_ref):
    length = mixed_ref.shape[1]
    width = mixed_ref.shape[2]
    pair = probs_ref.shape[3]
    low_half = lax.broadcasted_iota(jnp.int32, (length, pair), 1) < pair // 2
    live = live_ref[0] > 0.0
    for p in range(width // pair):
        query, key, value = (qkv_ref[0, :, s * width + p * pair : s * width + (p + 1) * pair] for s in range(3))
        scores = dot(split_pair(query, low_half), key, 1, 1) * scale
        bias = jnp.concatenate(
            [stat_ref[0, pl.ds(2 * p + s, length, stride=SLOTS), :] for s in range(2)], axis=0
        )
        scores = jnp.where(live, scores + bias, -1000000000.0)
        raised = jnp.exp(scores - jnp.max(scores, axis=1, keepdims=True))
        probs = raised / jnp.sum(raised, axis=1, keepdims=True)
        probs_ref[0, p] = probs
        mixed = dot(probs.astype(BF16), value, 1, 0)
        mixed_ref[0, :, p * pair : (p + 1) * pair] = jnp.where(low_half, mixed[:length], mixed[length:]).astype(BF16)


def attention_forward(qkv, stats, live, width, head_size):
    count, length, _ = qkv.shape
    pair = 2 * head_size
    pairs = width // pair
    return pl.pallas_call(
        lambda *refs: attention_forward_kernel(1.0 / math.sqrt(head_size), *refs),
        grid=(count,),
        in_specs=[
            pl.BlockSpec((1, length, 3 * width), lambda n: (n, 0, 0)),
            pl.BlockSpec((1, length * SLOTS, length), lambda n: (n, 0, 0)),
            pl.BlockSpec((1, 1, length), lambda n: (n, 0, 0)),
        ],
        out_specs=[
            pl.BlockSpec((1, pairs, 2 * length, length), lambda n: (n, 0, 0, 0)),
            pl.BlockSpec((1, length, width), lambda n: (n, 0, 0)),
        ],
        out_shape=[
            jax.ShapeDtypeStruct((count, pairs, 2 * length, length), F32),
            jax.ShapeDtypeStruct((count, length, width), BF16),
        ],
        compiler_params=pltpu.CompilerParams(vmem_limit_bytes=VMEM_BYTES),
        cost_estimate=pl.CostEstimate(flops=2 * count * pairs * 4 * length**3, bytes_accessed=6000000, transcendentals=0),
        name="attention_forward",
    )(qkv, stats.reshape(count, length * SLOTS, length), live)


def attention_backward_kernel(scale, qkv_ref, probs_ref, mixed_ref, out_ref, grad_ref):
    length = mixed_ref.shape[1]
    width = mixed_ref.shape[2]
    pair = probs_ref.shape[3]
    low_half = lax.broadcasted_iota(jnp.int32, (length, pair), 1) < pair // 2
    for p in range(width // pair):
        query, key, value = (qkv_ref[0, :, s * width + p * pair : s * width + (p + 1) * pair] for s in range(3))
        mixed = split_pair(mixed_ref[0, :, p * pair : (p + 1) * pair], low_half)
        probs = probs_ref[0, p]
        d_probs = dot(mixed, value, 1, 1)
        d_scores = (probs * (d_probs - jnp.sum(probs * d_probs, axis=1, keepdims=True))).astype(BF16)
        d_query = dot(d_scores, key, 1, 0) * scale
        parts = (
            jnp.where(low_half, d_query[:length], d_query[length:]),
            dot(d_scores, split_pair(query, low_half), 0, 0) * scale,
            dot(probs.astype(BF16), mixed, 0, 0),
        )
        for s in range(3):
            out_ref[0, :, s * width + p * pair : s * width + (p + 1) * pair] = parts[s].astype(BF16)
        wide = d_scores.astype(F32)
        for s in range(2):
            grad_ref[0, pl.ds(2 * p + s, length, stride=SLOTS), :] = wide[s * length : (s + 1) * length]


def attention_backward(qkv, probs, mixed, width, head_size):
    count, length, _ = qkv.shape
    pair = 2 * head_size
    pairs = width // pair
    d_qkv, d_scores = pl.pallas_call(
        lambda *refs: attention_backward_kernel(1.0 / math.sqrt(head_size), *refs),
        grid=(count,),
        in_specs=[
            pl.BlockSpec((1, length, 3 * width), lambda n: (n, 0, 0)),
            pl.BlockSpec((1, pairs, 2 * length, length), lambda n: (n, 0, 0, 0)),
            pl.BlockSpec((1, length, width), lambda n: (n, 0, 0)),
        ],
        out_specs=[
            pl.BlockSpec((1, length, 3 * width), lambda n: (n, 0, 0)),
            pl.BlockSpec((1, length * SLOTS, length), lambda n: (n, 0, 0)),
        ],
        out_shape=[
            jax.ShapeDtypeStruct((count, length, 3 * width), BF16),
            jax.ShapeDtypeStruct((count, length * SLOTS, length), F32),
        ],
        compiler_params=pltpu.CompilerParams(vmem_limit_bytes=VMEM_BYTES),
        cost_estimate=pl.CostEstimate(flops=2 * count * pairs * 8 * length**3, bytes_accessed=8000000, transcendentals=0),
        name="attention_backward",
    )(qkv, probs, mixed)
    return d_qkv, d_scores.reshape(count, length, SLOTS, length)


def normed_parts(values):
    center = values - jnp.mean(values, axis=-1, keepdims=True)
    inverse = lax.rsqrt(jnp.mean(center * center, axis=-1, keepdims=True) + EPS)
    return center * inverse, inverse


def normed_back(grad_hat, normed, inverse):
    return inverse * (
        grad_hat
        - jnp.mean(grad_hat, axis=-1, keepdims=True)
        - normed * jnp.mean(grad_hat * normed, axis=-1, keepdims=True)
    )


def one_hot(ids, size):
    return (lax.broadcasted_iota(jnp.int32, (ids.shape[0], size), 1) == ids[:, None]).astype(BF16)


def look_up(ids_cath, ids_time, cath_table, time_table):
    return dot(one_hot(ids_cath, cath_table.shape[0]), cath_table, 1, 0) + dot(
        one_hot(ids_time, time_table.shape[0]), time_table, 1, 0
    )


def shards(sizes, activations, pair_repr, cotangent, buckets, pad_mask, cath_ids, time_bins, *weights):
    (
        cath_table,
        time_table,
        cond_attn,
        cond_ffn,
        norm_attn,
        norm_ffn,
        pair_gain,
        qkv_weight,
        out_weight,
        pair_weight,
        gateup_weight,
        down_weight,
    ) = weights
    dp_size, fs_size = sizes
    chips = fs_size // 2
    count = activations.shape[0] * activations.shape[1]
    length, width = activations.shape[2:]
    channels = pair_repr.shape[4]
    heads = pair_weight.shape[1]
    head_size = width // heads
    share = width // fs_size
    slice_c = channels // fs_size
    hidden = down_weight.shape[0] * fs_size
    quarter = hidden // 4
    piece = down_weight.shape[0] // 4
    core = lax.axis_index("fsdp") % 2
    side = lax.axis_index("dp") % 2
    same_core = [[2 * g + c for g in range(chips)] for c in range(2)]
    swap_core = [(i, i ^ 1) for i in range(fs_size)]
    swap_side = [(i, i ^ 1) for i in range(dp_size)]

    def by_core(mine, other):
        return jnp.where(core == 0, mine, other), jnp.where(core == 0, other, mine)

    def to_core(values):
        return lax.ppermute(values, "fsdp", swap_core)

    def to_side(values):
        return lax.ppermute(values, "dp", swap_side)

    def by_side(mine, other):
        return jnp.where(side == 0, mine, other), jnp.where(side == 0, other, mine)

    x = activations.reshape(count, length, width).astype(F32)
    pair = pair_repr.reshape(count, length, length, channels)
    dy = cotangent.reshape(count, length, width).astype(F32)
    positions = lax.broadcasted_iota(jnp.int32, (count, length), 1)
    live = (positions < buckets.reshape(count, 1)) & (
        (pad_mask.reshape(count, length) == 1) | (positions == 0)
    )
    live_lane = live.astype(F32).reshape(count, 1, length)
    live_row = live.astype(F32).reshape(count, length, 1)
    ids = jnp.concatenate([cath_ids.reshape(count), time_bins.reshape(count)])

    small = jnp.concatenate(
        [
            norm_attn.astype(F32),
            norm_ffn.astype(F32),
            pair_gain.astype(F32),
            pair_weight.astype(F32).reshape(-1),
            ids.astype(F32),
        ]
    )
    small = lax.all_gather(small, "fsdp", axis=0, tiled=False)
    offsets = [0]
    for size in (share, share, slice_c, slice_c * heads, count, count):
        offsets.append(offsets[-1] + size)
    norm_attn_all, norm_ffn_all, gain_all, pairw_all, group_cath, group_time = (
        small[:, offsets[k] : offsets[k + 1]] for k in range(6)
    )
    norm_attn_all = norm_attn_all.reshape(1, 1, width)
    norm_ffn_all = norm_ffn_all.reshape(1, 1, width)
    gain_all = gain_all.reshape(channels, 1)
    pairw_all = pairw_all.reshape(channels, heads)

    attn_mine = jnp.concatenate([qkv_weight, out_weight], axis=1)
    attn_all = lax.all_gather(attn_mine, "fsdp", axis=0, tiled=True)
    qkv_all = attn_all[:, : 3 * width]
    out_all = attn_all[:, 3 * width :]
    gateup_parts = gateup_weight.reshape(share, 2, fs_size, 4, piece).transpose(3, 0, 1, 2, 4)
    ffn_parts = jnp.concatenate(
        [gateup_parts.reshape(4, share, 2 * quarter), down_weight.reshape(4, piece, width)], axis=2
    )
    ffn_mine = lax.dynamic_index_in_dim(ffn_parts, 2 * side + core, 0, keepdims=False)
    ffn_other = to_core(lax.dynamic_index_in_dim(ffn_parts, 2 * side + 1 - core, 0, keepdims=False))
    ffn_chip = jnp.concatenate(by_core(ffn_mine, ffn_other), axis=0)
    ffn_all = lax.all_gather(ffn_chip, "fsdp", axis=0, tiled=True, axis_index_groups=same_core)
    gateup_all = ffn_all[:, : 2 * quarter]
    down_all = ffn_all[:, 2 * quarter :]

    raw = look_up(
        group_cath.reshape(-1).astype(jnp.int32), group_time.reshape(-1).astype(jnp.int32), cath_table, time_table
    )
    cond_mine = jnp.concatenate([cond_attn, cond_ffn], axis=1)
    terms = dot(jax.nn.silu(raw).astype(BF16), cond_mine, 1, 0)
    mod = lax.all_to_all(terms, "fsdp", 0, 0, tiled=True)
    mod = jnp.sum(mod.reshape(fs_size, count, 6 * width), axis=0)
    shift_attn, scale_attn, gate_attn, shift_ffn, scale_ffn, gate_ffn = (
        mod[:, None, k * width : (k + 1) * width] for k in range(6)
    )

    eye = lax.broadcasted_iota(jnp.int32, (channels, channels), 0) == lax.broadcasted_iota(
        jnp.int32, (channels, channels), 1
    )
    center = (eye.astype(F32) - 1.0 / channels).astype(BF16)
    gained = gain_all * pairw_all
    bias_weight = jnp.pad(gained.astype(BF16), ((0, 0), (0, length - heads)))
    square_weight = jnp.where(
        lax.broadcasted_iota(jnp.int32, (channels, length), 1) == SLOTS - 1, 1.0 / channels, 0.0
    ).astype(BF16)
    stats = pair_forward(pair, center, bias_weight, square_weight)

    attn_hat, attn_inv = normed_parts(x)
    normed_attn = (attn_hat * norm_attn_all * (1.0 + scale_attn) + shift_attn).astype(BF16)
    rows = count * length
    normed_attn_rows = normed_attn.reshape(rows, width)
    qkv = dot(normed_attn_rows, qkv_all, 1, 0).astype(BF16).reshape(count, length, 3 * width)
    probs, mixed = attention_forward(qkv, stats, live_lane, width, head_size)
    mixed_rows = mixed.reshape(rows, width)
    branch_attn = dot(mixed_rows, out_all, 1, 0).reshape(count, length, width)
    after = x + gate_attn * live_row * branch_attn
    ffn_hat, ffn_inv = normed_parts(after)
    normed_ffn = (ffn_hat * norm_ffn_all * (1.0 + scale_ffn) + shift_ffn).astype(BF16).reshape(rows, width)
    d_branch_ffn = (gate_ffn * live_row * dy).astype(BF16).reshape(rows, width)

    def spread_rows(values):
        both = jnp.stack(by_side(values, to_side(values)))
        return jnp.stack(by_core(both, to_core(both))).reshape(4 * rows, width)

    def sum_rows(values):
        parts = values.reshape(2, 2, rows, width)
        keep = lax.dynamic_index_in_dim(parts, core, 0, keepdims=False)
        away = lax.dynamic_index_in_dim(parts, 1 - core, 0, keepdims=False)
        chip = keep + to_core(away.astype(BF16)).astype(F32)
        keep = lax.dynamic_index_in_dim(chip, side, 0, keepdims=False)
        away = lax.dynamic_index_in_dim(chip, 1 - side, 0, keepdims=False)
        return (keep + to_side(away.astype(BF16)).astype(F32)).reshape(count, length, width)

    normed_four = spread_rows(normed_ffn)
    d_branch_four = spread_rows(d_branch_ffn)
    gate_up = dot(normed_four, gateup_all, 1, 0).astype(BF16).astype(F32)
    gate_part = gate_up[:, :quarter]
    up_part = gate_up[:, quarter:]
    sigma = jax.nn.sigmoid(gate_part)
    silu = gate_part * sigma
    hidden_low = (silu * up_part).astype(BF16)
    branch_part = dot(hidden_low, down_all, 1, 0)
    d_hidden = dot(d_branch_four, down_all, 1, 1)
    d_gate_up = jnp.concatenate(
        [d_hidden * up_part * (sigma * (1.0 + gate_part * (1.0 - sigma))), d_hidden * silu], axis=1
    ).astype(BF16)
    d_normed_ffn = sum_rows(dot(d_gate_up, gateup_all, 1, 1))
    branch_ffn = sum_rows(branch_part)
    ffn_grads = jnp.concatenate(
        [
            dot(normed_four, d_gate_up, 0, 0).astype(BF16),
            dot(hidden_low, d_branch_four, 0, 0).astype(BF16),
        ],
        axis=1,
    )
    ffn_grads = lax.psum_scatter(
        ffn_grads, "fsdp", scatter_dimension=0, tiled=True, axis_index_groups=same_core
    )

    block_out = (after + gate_ffn * live_row * branch_ffn).astype(BF16)
    d_gate_ffn = jnp.sum(live_row * branch_ffn * dy, axis=1)
    d_shift_ffn = jnp.sum(d_normed_ffn, axis=1)
    ffn_dot = jnp.sum(d_normed_ffn * ffn_hat, axis=1)
    d_scale_ffn = ffn_dot * norm_ffn_all[0]
    d_norm_ffn = jnp.sum(ffn_dot * (1.0 + scale_ffn[:, 0]), axis=0)
    d_after = dy + normed_back(d_normed_ffn * norm_ffn_all * (1.0 + scale_ffn), ffn_hat, ffn_inv)

    d_branch_attn = (gate_attn * live_row * d_after).astype(BF16).reshape(rows, width)
    d_gate_attn = jnp.sum(live_row * branch_attn * d_after, axis=1)
    d_mixed = dot(d_branch_attn, out_all, 1, 1).astype(BF16).reshape(count, length, width)
    d_qkv, d_scores = attention_backward(qkv, probs, d_mixed, width, head_size)
    d_qkv_rows = d_qkv.reshape(rows, 3 * width)
    attn_grads = jnp.concatenate(
        [
            dot(normed_attn_rows, d_qkv_rows, 0, 0).astype(BF16),
            dot(mixed_rows, d_branch_attn, 0, 0).astype(BF16),
        ],
        axis=1,
    )
    attn_grads = lax.psum_scatter(attn_grads, "fsdp", scatter_dimension=0, tiled=True)
    d_normed_attn = dot(d_qkv_rows, qkv_all, 1, 1).reshape(count, length, width)
    d_shift_attn = jnp.sum(d_normed_attn, axis=1)
    attn_dot = jnp.sum(d_normed_attn * attn_hat, axis=1)
    d_scale_attn = attn_dot * norm_attn_all[0]
    d_norm_attn = jnp.sum(attn_dot * (1.0 + scale_attn[:, 0]), axis=0)
    grad_input = (
        d_after + normed_back(d_normed_attn * norm_attn_all * (1.0 + scale_attn), attn_hat, attn_inv)
    ).astype(BF16)

    spread = gained - jnp.mean(gained, axis=0, keepdims=True)
    spread = jnp.concatenate(
        [
            jnp.pad(spread.T, ((0, SLOTS - heads), (0, 0))),
            jnp.where(
                lax.broadcasted_iota(jnp.int32, (SLOTS, channels), 0) // 2 == heads // 2, 1.0, 0.0
            ),
        ],
        axis=1,
    ).astype(BF16)
    spread = jnp.tile(spread, (length // SLOTS, 1))
    grad_pair, pair_sum = pair_backward(heads, pair, d_scores, stats, center, spread)

    message = jnp.concatenate(
        [
            jnp.concatenate(
                [d_shift_attn, d_scale_attn, d_gate_attn, d_shift_ffn, d_scale_ffn, d_gate_ffn], axis=1
            ).reshape(-1),
            d_norm_attn,
            d_norm_ffn,
            pair_sum[:heads].reshape(-1),
            (ids // 32).astype(F32),
            (ids % 32).astype(F32),
        ]
    ).astype(BF16)
    message = lax.all_gather(message, EVERY, axis=0, tiled=False)
    cut = count * 6 * width
    d_mod = message[:, :cut].reshape(-1, 6 * width)
    rest = message[:, cut:].astype(F32)
    all_ids = (rest[:, -4 * count : -2 * count] * 32.0 + rest[:, -2 * count :]).astype(jnp.int32)
    all_cath = all_ids[:, :count].reshape(-1)
    all_time = all_ids[:, count:].reshape(-1)
    sums = jnp.sum(rest[:, : 2 * width + heads * channels], axis=0)
    me = lax.axis_index("fsdp")
    grad_norm_attn = lax.dynamic_slice_in_dim(sums[:width], me * share, share)
    grad_norm_ffn = lax.dynamic_slice_in_dim(sums[width : 2 * width], me * share, share)
    pair_sums = sums[2 * width :].reshape(heads, channels).T
    grad_pairw = lax.dynamic_slice_in_dim(pair_sums * gain_all, me * slice_c, slice_c)
    grad_gain = lax.dynamic_slice_in_dim(jnp.sum(pair_sums * pairw_all, axis=1), me * slice_c, slice_c)
    raw_all = look_up(all_cath, all_time, cath_table, time_table)
    grad_cond = dot(jax.nn.silu(raw_all).astype(BF16), d_mod, 0, 0)
    sigma_all = jax.nn.sigmoid(raw_all)
    d_cond = dot(d_mod, cond_mine, 1, 1) * (sigma_all * (1.0 + raw_all * (1.0 - sigma_all)))

    def table_grad(all_of, size):
        hot = one_hot(all_of, size).astype(F32)
        return lax.dot_general(hot, d_cond, (((0,), (0,)), ((), ())), precision=lax.Precision.HIGHEST)

    grad_cath = table_grad(all_cath, cath_table.shape[0])
    grad_time = table_grad(all_time, time_table.shape[0])

    def over_dp(values):
        if dp_size == 2:
            return values.astype(F32) + to_side(values).astype(F32)
        return lax.psum(values, "dp").astype(F32)

    attn_grads = over_dp(attn_grads)
    ffn_rows = ffn_grads.reshape(2, share, 2 * quarter + width)
    keep = lax.dynamic_index_in_dim(ffn_rows, core, 0, keepdims=False)
    away = lax.dynamic_index_in_dim(ffn_rows, 1 - core, 0, keepdims=False)
    halves = jnp.stack(by_core(keep, to_core(away)))
    if dp_size == 2:
        fours = jnp.stack(by_side(halves, to_side(halves))).astype(F32)
    else:
        fours = lax.all_gather(halves, "dp", axis=0, tiled=False).astype(F32)
        fours = jnp.sum(fours.reshape((dp_size // 2, 2) + halves.shape), axis=0)
    fours = fours.reshape(4, share, 2 * quarter + width)
    grad_gateup = (
        fours[:, :, : 2 * quarter].reshape(4, share, 2, fs_size, piece).transpose(1, 2, 3, 0, 4).reshape(share, 2 * hidden)
    )
    grad_down = fours[:, :, 2 * quarter :].reshape(4 * piece, width)

    return (
        block_out.reshape(activations.shape),
        grad_input.reshape(activations.shape),
        grad_pair.reshape(pair_repr.shape),
        grad_cath,
        grad_time,
        grad_cond[:, : 3 * width],
        grad_cond[:, 3 * width :],
        grad_norm_attn,
        grad_norm_ffn,
        grad_gain,
        attn_grads[:, : 3 * width],
        attn_grads[:, 3 * width :],
        grad_pairw,
        grad_gateup,
        grad_down,
    )


def solution(mesh):
    chains = ("dp", "fsdp")
    in_specs = (
        P(None, chains, None, None),
        P(None, chains, None, None, None),
        P(None, chains, None, None),
        P(None, chains),
        P(None, chains, None),
        P(None, chains),
        P(None, chains),
        P(None, "fsdp"),
        P(None, "fsdp"),
        P("fsdp", None),
        P("fsdp", None),
        P("fsdp"),
        P("fsdp"),
        P("fsdp"),
        P("fsdp", None),
        P("fsdp", None),
        P("fsdp", None),
        P("fsdp", None),
        P("fsdp", None),
    )
    out_specs = (
        P(None, chains, None, None),
        P(None, chains, None, None),
        P(None, chains, None, None, None),
        P(None, "fsdp"),
        P(None, "fsdp"),
        P("fsdp", None),
        P("fsdp", None),
        P("fsdp"),
        P("fsdp"),
        P("fsdp"),
        P("fsdp", None),
        P("fsdp", None),
        P("fsdp", None),
        P("fsdp", None),
        P("fsdp", None),
    )
    sizes = (mesh.shape["dp"], mesh.shape["fsdp"])
    return jax.shard_map(
        lambda *args: shards(sizes, *args), mesh=mesh, in_specs=in_specs, out_specs=out_specs, check_vma=False
    )
```

time: 1870 us -> 404 us (0.22)
  waiting for transfers between devices: 1400 us -> 92.3 us
  matrix products: 193 us -> 32.2 us
  other arithmetic: 114 us -> 35.5 us
  Pallas kernels: 0 us -> 52.8 us
    reduce_scatter x18 -> x2, waiting for transfers between devices: 1070 us -> 48.7 us  [the longest x1 48.7 us: shards(): lax.psum_scatter(attn_grads, 'fsdp', scatter_dimension=0, tiled=True)]
    all_gather x8 -> x2, waiting for transfers between devices: 231 us -> 8.23 us  [the longest x1 8.23 us: shards(): lax.all_gather(ffn_chip, 'fsdp', axis=0, tiled=True, axis_index_groups=sa...]
    dot_general x54 -> x20, matrix products: 193 us -> 32.2 us  [the longest x18 30.2 us: dot(): lax.dot_general(a, b, (((a_dim,), (b_dim,)), ((), ())), preferred_element...]
    psum x1 -> x0, waiting for transfers between devices: 90.3 us -> none  [shards(): lax.psum(owned[0].astype(jnp.bfloat16), 'dp').astype(jnp.float32)]
    pallas_call x0 -> x4, Pallas kernels: none -> 52.8 us  [the longest x1 24.6 us: pair_backward(): pl.pallas_call(lambda *refs: pair_backward_kernel(heads, *refs), grid=(co...]
    ppermute x0 -> x12, waiting for transfers between devices: none -> 35.3 us  [the longest x6 34.2 us: to_side(): return lax.ppermute(values, 'dp', swap_side)]
    all_gather x1, blocking collectives: 17.7 us -> 47.3 us  [shards(): message = lax.all_gather(message, EVERY, axis=0, tiled=False)]
    convert_element_type x18 -> x12, other arithmetic: 24 us -> 4.35 us  [the longest x1 1.04 us: shards(): (attn_hat * norm_attn_all * (1.0 + scale_attn) + shift_attn).astype(BF16)]
  transfers between devices with their start and end apart: 27 -> 17, of which waited for: 22 -> 7; matrix products, arithmetic and copies ran while one was open for 15% -> 23% of each run, Pallas kernels for 0% -> 13%
where the time goes in v1:
time: 404 us; the launch traced here: 398 us
  blocking collectives  111 us (27%)
  waiting for transfers between devices  92.3 us (23%)
  Pallas kernels  52.8 us (13%)
  local copies, waits for them, and re-layouts  46.2 us (11%)
  other arithmetic  35.5 us (9%)
  matrix products  32.2 us (8%)
  between operations  16.1 us (4%)
  starting transfers between devices  12 us (3%)
    unnamed x1, blocking collectives  63.7 us
    reduce_scatter x1, waiting for transfers between devices, shards(): lax.psum_scatter(attn_grads, 'fsdp', scatter_dimension=0, tiled=True)  48.7 us
    all_gather x1, blocking collectives, shards(): message = lax.all_gather(message, EVERY, axis=0, tiled=False)  47.3 us
    ppermute x6, waiting for transfers between devices, to_side(): return lax.ppermute(values, 'dp', swap_side)  34.2 us
    dot_general x18, matrix products, dot(): lax.dot_general(a, b, (((a_dim,), (b_dim,)), ((), ())), preferred_element...  30.2 us
    pallas_call x1, Pallas kernels, pair_backward(): pl.pallas_call(lambda *refs: pair_backward_kernel(heads, *refs), grid=(co...  24.6 us
    pallas_call x1, Pallas kernels, pair_forward(): pl.pallas_call(pair_forward_kernel, grid=(count, length // rows), in_spec...  20.9 us
    reshape x3, local copies, waits for them, and re-layouts, shards(): fours[:, :, :2 * quarter].reshape(4, share, 2, fs_size, piece)  12.9 us
  transfers between devices with their start and end apart: 17, of which 7 were waited for; matrix products, arithmetic and copies ran while one was open for 23% of the time, Pallas kernels for 13%

profile of v1, /device:TPU:0, one launch (start us, length us, event | category | flops | bytes accessed | tf_op | source)
XLA Modules:
  0.0 398.2 jit_solution(6438370652214081704)
XLA Ops:
  15.8 63.7 %all-reduce.2 = f32[4928]{0:T(1024)S(1)} all-reduce(f32[4928]{0:T(1024)S(1)} %dynamic-update-slice), channel_id=2, replica_groups=mesh['dp'=2,'fsdp'=16] {'fsdp'}, use_global_device_ids=true, to_apply=%add.2 | all-reduce | flops 4928 | bytes 39424
  84.9 4.2 %all-to-all-start = ((f32[16,2,4608]{2,1,0:T(2,128)}), f32[16,2,4608]{2,1,0:T(2,128)}, u32[]{:S(2)}, u32[]{:S(2)}) async-start(f32[16,2,4608]{2,1,0:T(2,128)} %all_to_all.6), calls=%async_computation | async-start | bytes 1179648 | tf_op jit(solution)/shard_map/all_to_all | solution.py:348
  89.2 2.5 reshape.518
  92.1 2.8 reshape.519
  99.8 20.9 %pair_forward.1.refs_2_ = f32[2,128,16,128]{3,2,1,0:T(8,128)S(1)} custom-call(bf16[2,128,128,256]{3,2,1,0:T(8,128)(2,1)} %bitcast.317, bf16[256,256]{1,0:T(8,128)(2,1)S(1)} %add_convert_fusion.2.center_ref.refs_3_, bf16[256,128]{1,0:T(8,128)(2,1)S(1)} %pad.9.weight_ref, bf16[256,128]{1,0:T(8,128)(2,1)S(1)} %iota.85.square_ref), custom_call_target="tpu_custom_call" | custom-call | flops 12884901888 | bytes 16777216 | tf_op jit(solution)/shard_map/pair_forward/pallas_call | solution.py:42
  125.9 3.2 convolution_convert_fusion
  131.4 3.3 fusion.94
  138.4 7.9 %collective-permute-done = bf16[256,768]{1,0:T(8,128)(2,1)S(1)} collective-permute-done((bf16[256,768]{1,0:T(8,128)(2,1)S(1)}, bf16[256,768]{1,0:T(8,128)(2,1)S(1)}, u32[]{:S(2)}, u32[]{:S(2)}) %collective-permute-start) | collective-permute-done | bytes 393248 | tf_op jit(solution)/shard_map/ppermute | solution.py:291
  157.1 8.2 %all-gather.7.cloned.1.call-done = bf16[768,2304]{1,0:T(8,128)(2,1)} async-done(((bf16[96,2304]{1,0:T(8,128)(2,1)}), bf16[768,2304]{1,0:T(8,128)(2,1)}) %all-gather.7.cloned.1.call-update) | async-done | bytes 3538960 | tf_op jit(solution)/shard_map/all_gather | solution.py:339
  165.4 4.9 %fusion = f32[1024,1536]{1,0:T(8,128)S(1)} fusion(bf16[1024,768]{1,0:T(8,128)(2,1)} %bitcast.296, bf16[768,2304]{1,0:T(8,128)(2,1)} %all-gather.7.cloned.1.call-done), kind=kOutput, calls=%fused_computation.4 | convolution fusion | flops 2419064832 | bytes 10223616 | tf_op jit(solution)/shard_map/dot_general | solution.py:18
  170.3 3.1 multiply_convert_fusion.1
  176.6 3.3 convolution_convert_fusion.2
  179.9 2.6 fusion.6
  194.4 8.4 %collective-permute-done.8 = bf16[256,768]{1,0:T(8,128)(2,1)S(1)} collective-permute-done((bf16[256,768]{1,0:T(8,128)(2,1)S(1)}, bf16[256,768]{1,0:T(8,128)(2,1)S(1)}, u32[]{:S(2)}, u32[]{:S(2)}) %collective-permute-start.8) | collective-permute-done | bytes 393248 | tf_op jit(solution)/shard_map/ppermute | solution.py:291
  203.5 7.4 %collective-permute-done.4 = bf16[256,768]{1,0:T(8,128)(2,1)S(1)} collective-permute-done((bf16[256,768]{1,0:T(8,128)(2,1)S(1)}, bf16[256,768]{1,0:T(8,128)(2,1)S(1)}, u32[]{:S(2)}, u32[]{:S(2)}) %collective-permute-start.4) | collective-permute-done | bytes 393248 | tf_op jit(solution)/shard_map/ppermute | solution.py:291
  214.5 5.2 %attention_backward.1 = (bf16[2,128,2304]{2,1,0:T(8,128)(2,1)S(1)}, f32[2,2048,128]{2,1,0:T(8,128)}) custom-call(bf16[2,128,2304]{2,1,0:T(8,128)(2,1)S(1)} %bitcast.279, f32[2,6,256,128]{3,2,1,0:T(8,128)S(1)} %copy-done.2, bf16[2,128,768]{2,1,0:T(8,128)(2,1)S(1)} %bitcast.281), custom_call_target="tpu_custom_call" | custom-call | flops 402653184 | bytes 8000000 | tf_op jit(solution)/shard_map/attention_backward/pallas_call | solution.py:204
  222.8 24.6 %pair_backward.1 = (bf16[2,128,128,256]{3,2,1,0:T(8,128)(2,1)}, f32[16,256]{1,0:T(8,128)S(1)}) custom-call(bf16[2,128,128,256]{3,2,1,0:T(8,128)(2,1)} %bitcast.318, f32[2,128,16,128]{3,2,1,0:T(8,128)S(1)} %bitcast.283, f32[2,128,16,128]{3,2,1,0:T(8,128)S(1)} %pair_forward.1.refs_2_, bf16[256,256]{1,0:T(8,128)(2,1)S(1)} %add_convert_fusion.2.center_ref.refs_3_, ...), custom_call_target="tpu_custom_call" | custom-call | flops 17179869184 | bytes 33554432 | tf_op jit(solution)/shard_map/pair_backward/pallas_call | solution.py:102
  247.6 47.3 %all-gather.1 = bf16[32,1,13832]{2,1,0:T(2,128)(2,1)S(1)} all-gather(bf16[1,1,13832]{2,1,0:T(2,128)(2,1)S(1)} %bitcast.308), channel_id=1, replica_groups=mesh['dp'=2,'fsdp'=16] {'dp','fsdp'}, dimensions={0}, use_global_device_ids=true | all-gather | bytes 912912 | tf_op jit(solution)/shard_map/all_gather | solution.py:472
  297.8 2.8 pad_maximum_fusion
  313.7 10.5 %collective-permute-done.11 = bf16[2,48,2304]{2,1,0:T(8,128)(2,1)S(1)} collective-permute-done((bf16[2,48,2304]{2,1,0:T(8,128)(2,1)S(1)}, bf16[2,48,2304]{2,1,0:T(8,128)(2,1)S(1)}, u32[]{:S(2)}, u32[]{:S(2)}) %collective-permute-start.11) | collective-permute-done | bytes 442400 | tf_op jit(solution)/shard_map/ppermute | solution.py:291
  324.4 48.7 %reduce-scatter.3.cloned.1.call-done = bf16[48,3072]{1,0:T(8,128)(2,1)} async-done(((bf16[768,3072]{1,0:T(8,128)(2,1)}), bf16[48,3072]{1,0:T(8,128)(2,1)}) %reduce-scatter.3.cloned.1.call-update) | async-done | bytes 294928 | tf_op jit(solution)/shard_map/reduce_scatter | solution.py:437
  376.8 2.4 reshape.534
  379.2 4.5 %copy.107 = f32[4,48,2,16,48]{4,0,3,2,1:T(4,128)} copy(f32[4,48,2,16,48]{4,3,2,1,0:T(8,128)S(1)} %reshape.534) | data formatting | bytes 2359296 | tf_op jit(solution)/shard_map/reshape | solution.py:515
  383.7 6.0 %reshape.535 = f32[48,6144]{1,0:T(8,128)} reshape(f32[48,2,16,4,48]{4,3,2,1,0:T(4,128)} %bitcast.284) | data formatting | bytes 2359296 | tf_op jit(solution)/shard_map/reshape | solution.py:515
  (295 shorter events, 83.7 us)
Async XLA Ops:
  7.2 76.1 %copy-start = (bf16[1000,48]{0,1:T(8,128)(2,1)S(1)}, bf16[1000,48]{0,1:T(8,128)(2,1)}, u32[]{:S(2)}) copy-start(bf16[1000,48]{0,1:T(8,128)(2,1)} %param.27) | copy-start | bytes 288004
  7.2 118.7 %all-gather.5.cloned.1.call-start = ((), (), s32[]{:S(2)}) async-start(), calls=%async_computation.3 | async-start | bytes 5013504 | tf_op jit(solution)/shard_map/all_gather | solution.py:329
  84.9 35.8 %all-to-all-start = ((f32[16,2,4608]{2,1,0:T(2,128)}), f32[16,2,4608]{2,1,0:T(2,128)}, u32[]{:S(2)}, u32[]{:S(2)}) async-start(f32[16,2,4608]{2,1,0:T(2,128)} %all_to_all.6), calls=%async_computation | async-start | bytes 1179648 | tf_op jit(solution)/shard_map/all_to_all | solution.py:348
  89.1 76.2 %all-gather.7.cloned.1.call-start = ((), (), s32[]{:S(2)}) async-start(), calls=%async_computation.4 | async-start | bytes 3981312 | tf_op jit(solution)/shard_map/all_gather | solution.py:339
  95.0 2.8 collective-permute-start.2
  98.7 209.5 %reduce-scatter.5.cloned.1.call-start = ((), (), s32[]{:S(2)}) async-start(), calls=%async_computation.6 | async-start | bytes 3981312 | tf_op jit(solution)/shard_map/reduce_scatter | solution.py:413
  98.9 197.6 %copy-start.46 = (f32[2,128]{1,0:T(2,128)}, f32[2,128]{1,0:T(2,128)S(1)}, u32[]{:S(2)}) copy-start(f32[2,128]{1,0:T(2,128)S(1)} %get-tuple-element.143) | copy-start | bytes 3076
  99.8 22.8 %copy-start.32 = (bf16[2,1,128,768]{3,2,1,0:T(8,128)(2,1)S(1)}, bf16[2,1,128,768]{3,2,1,0:T(8,128)(2,1)}, u32[]{:S(2)}) copy-start(bf16[2,1,128,768]{3,2,1,0:T(8,128)(2,1)} %param.21) | copy-start | bytes 1179652
  99.8 25.0 %copy-start.54 = (f32[256]{0:T(256)S(1)}, f32[256]{0:T(256)}, u32[]{:S(2)}) copy-start(f32[256]{0:T(256)} %get-tuple-element.148) | copy-start | bytes 3076
  123.5 12.6 %collective-permute-start.5 = (bf16[256,768]{1,0:T(8,128)(2,1)}, bf16[256,768]{1,0:T(8,128)(2,1)}, u32[]{:S(2)}, u32[]{:S(2)}) collective-permute-start(bf16[256,768]{1,0:T(8,128)(2,1)} %fusion.23), channel_id=1, source_target_pairs={{0,16},{16,0},{1,17},{17,1},{2,18},{18,2},{3,19},{19,3},{4,20},{20... | collective-permute-start | bytes 1179656 | tf_op jit(solution)/shard_map/ppermute | solution.py:291
  135.3 11.1 %collective-permute-start = (bf16[256,768]{1,0:T(8,128)(2,1)S(1)}, bf16[256,768]{1,0:T(8,128)(2,1)S(1)}, u32[]{:S(2)}, u32[]{:S(2)}) collective-permute-start(bf16[256,768]{1,0:T(8,128)(2,1)S(1)} %bitcast.298), channel_id=1, source_target_pairs={{0,16},{16,0},{1,17},{17,1},{2,18},{18,2},{3,19},{19,3},{4,20},{20... | collective-permute-start | bytes 1179656 | tf_op jit(solution)/shard_map/ppermute | solution.py:291
  138.4 14.0 %collective-permute-start.6 = (bf16[2,256,768]{2,1,0:T(8,128)(2,1)}, bf16[2,256,768]{2,1,0:T(8,128)(2,1)}, u32[]{:S(2)}, u32[]{:S(2)}) collective-permute-start(bf16[2,256,768]{2,1,0:T(8,128)(2,1)} %pad_maximum_fusion.9), channel_id=1, source_target_pairs={{0,1},{1,0},{2,3},{3,2},{4,5},{5,4},{6,7},{7,6},{8,9},{9,8},{10,11... | collective-permute-start | bytes 2359304 | tf_op jit(solution)/shard_map/ppermute | solution.py:288
  148.2 4.2 %collective-permute-start.1 = (bf16[2,256,768]{2,1,0:T(8,128)(2,1)}, bf16[2,256,768]{2,1,0:T(8,128)(2,1)}, u32[]{:S(2)}, u32[]{:S(2)}) collective-permute-start(bf16[2,256,768]{2,1,0:T(8,128)(2,1)} %pad_maximum_fusion.8), channel_id=1, source_target_pairs={{0,1},{1,0},{2,3},{3,2},{4,5},{5,4},{6,7},{7,6},{8,9},{9,8},{10,11... | collective-permute-start | bytes 2359304 | tf_op jit(solution)/shard_map/ppermute | solution.py:288
  175.9 16.3 %collective-permute-start.3 = (bf16[2,256,768]{2,1,0:T(8,128)(2,1)}, bf16[2,256,768]{2,1,0:T(8,128)(2,1)}, u32[]{:S(2)}, u32[]{:S(2)}) collective-permute-start(bf16[2,256,768]{2,1,0:T(8,128)(2,1)} %fusion.19), channel_id=1, source_target_pairs={{0,1},{1,0},{2,3},{3,2},{4,5},{5,4},{6,7},{7,6},{8,9},{9,8},{10,11... | collective-permute-start | bytes 2359304 | tf_op jit(solution)/shard_map/ppermute | solution.py:288
  185.2 3.6 collective-permute-start.7
  188.7 184.3 %reduce-scatter.3.cloned.1.call-start = ((), (), s32[]{:S(2)}) async-start(), calls=%async_computation.5 | async-start | bytes 5013504 | tf_op jit(solution)/shard_map/reduce_scatter | solution.py:437
  190.8 12.0 %collective-permute-start.8 = (bf16[256,768]{1,0:T(8,128)(2,1)S(1)}, bf16[256,768]{1,0:T(8,128)(2,1)S(1)}, u32[]{:S(2)}, u32[]{:S(2)}) collective-permute-start(bf16[256,768]{1,0:T(8,128)(2,1)S(1)} %fusion.47), channel_id=1, source_target_pairs={{0,16},{16,0},{1,17},{17,1},{2,18},{18,2},{3,19},{19,3},{4,20},{20... | collective-permute-start | bytes 1179656 | tf_op jit(solution)/shard_map/ppermute | solution.py:291
  193.5 17.3 %copy-start.20 = (f32[2,128,768]{2,1,0:T(8,128)S(1)}, f32[2,128,768]{2,1,0:T(8,128)}, u32[]{:S(2)}) copy-start(f32[2,128,768]{2,1,0:T(8,128)} %get-tuple-element.152) | copy-start | bytes 2359300
  193.6 17.3 %collective-permute-start.4 = (bf16[256,768]{1,0:T(8,128)(2,1)S(1)}, bf16[256,768]{1,0:T(8,128)(2,1)S(1)}, u32[]{:S(2)}, u32[]{:S(2)}) collective-permute-start(bf16[256,768]{1,0:T(8,128)(2,1)S(1)} %fusion.45), channel_id=1, source_target_pairs={{0,16},{16,0},{1,17},{17,1},{2,18},{18,2},{3,19},{19,3},{4,20},{20... | collective-permute-start | bytes 1179656 | tf_op jit(solution)/shard_map/ppermute | solution.py:291
  222.8 24.6 %copy-start.55 = (bf16[1,4]{1,0:T(2,128)(2,1)S(1)}, bf16[1,4]{1,0:T(2,128)(2,1)}, u32[]{:S(2)}) copy-start(bf16[1,4]{1,0:T(2,128)(2,1)} %get-tuple-element.98) | copy-start | bytes 28
  222.8 24.6 %copy-start.57 = (bf16[1,4]{1,0:T(2,128)(2,1)S(1)}, bf16[1,4]{1,0:T(2,128)(2,1)}, u32[]{:S(2)}) copy-start(bf16[1,4]{1,0:T(2,128)(2,1)} %get-tuple-element.150) | copy-start | bytes 28
  309.1 1.5 collective-permute-start.10
  311.7 12.5 %collective-permute-start.11 = (bf16[2,48,2304]{2,1,0:T(8,128)(2,1)S(1)}, bf16[2,48,2304]{2,1,0:T(8,128)(2,1)S(1)}, u32[]{:S(2)}, u32[]{:S(2)}) collective-permute-start(bf16[2,48,2304]{2,1,0:T(8,128)(2,1)S(1)} %pad_maximum_fusion.11), channel_id=1, source_target_pairs={{0,16},{16,0},{1,17},{17,1},{2,18},{18,2},{3,19},{19,3},{4,20},{20... | collective-permute-start | bytes 1327112 | tf_op jit(solution)/shard_map/ppermute | solution.py:291
  373.1 16.6 %collective-permute-start.9 = (bf16[48,3072]{1,0:T(8,128)(2,1)}, bf16[48,3072]{1,0:T(8,128)(2,1)S(1)}, u32[]{:S(2)}, u32[]{:S(2)}) collective-permute-start(bf16[48,3072]{1,0:T(8,128)(2,1)} %reduce-scatter.3.cloned.1.call-done), channel_id=1, source_target_pairs={{0,16},{16,0},{1,17},{17,1},{2,18},{18,2},{3,19},{19,3},{4,20},{20... | collective-permute-start | bytes 884744 | tf_op jit(solution)/shard_map/ppermute | solution.py:291
  (56 other events, 224.8 us)
Sparse Core Ops, SparseCore 0:
  10.9 56.5 all-gather.4
  98.8 66.5 all-gather.6
  188.9 82.4 reduce-scatter.4
  300.8 72.2 reduce-scatter.2
